TPU v7x, 32 devices: a whole 2x2x4 slice. The times are simulated.
32 devices in a mesh: conf: 2 (over x), virt: 16 (over z, y, core).
Axes of the slice: x: 2, y: 2, z: 4, core: 2. Of those that a mesh axis runs over, the one named last changes fastest.
Arguments:
- i_factors: float32 [32, 1024, 2048], P('conf', 'virt'), parts along dimension 0, may hold values from -0.6 to 0.6
- j_factors: float32 [4, 1024, 2048], P('conf', 'virt'), parts along dimension 0, may hold values from -0.6 to 0.6
- occ_i: float32 [32], P('conf'), parts along dimension 0, may hold values from -2 to -0.3
- occ_j: float32 [4], P('conf'), parts along dimension 0, may hold values from -2 to -0.3
- virt_energy: float32 [2048], P(('conf', 'virt')), parts along dimension 0, may hold values from 0.3 to 3
Outputs:
- density: float32 [32, 1024, 2048], P('conf', 'virt'), parts along dimension 0
There are 2 independent parts, one for each index of `conf`. A program takes and returns all parts, laid end to end along the dimension named above; each array names one. Nothing has to cross between parts.
All inputs are finite; a program needn't handle non-finite values.
Results may differ from a plain program's by a relative error of at most 0.00005.
Values sent between devices are 32-bit elements; how exact they have to be, the bound alone decides.
A program may use at most 128 MiB of HBM per device.

v0:
```python
import jax
import jax.numpy as jnp
from jax import lax
from jax.sharding import PartitionSpec as P


def transpose_blocks(pair_block, blocks):
    leading = pair_block.shape[:-2]
    height = pair_block.shape[-2]
    width = pair_block.shape[-1]
    split = pair_block.reshape(leading + (height, blocks, height))
    moved = jnp.swapaxes(split, -1, -3)
    return moved.reshape(leading + (height, width))


def body(i_factors, j_factors, occ_i, occ_j, virt_energy):
    blocks = lax.axis_size("virt")
    left_rows = i_factors.reshape(-1, i_factors.shape[2])
    density = jnp.zeros(i_factors.shape, jnp.float32)
    for index in range(j_factors.shape[0]):
        whole_rows, whole_energy = (
            lax.all_gather(j_factors[index], "virt", axis=0, tiled=True),
            lax.all_gather(virt_energy, "virt", axis=0, tiled=True),
        )
        pair_block = jnp.dot(left_rows, whole_rows.T, precision=lax.Precision.HIGHEST)
        pair_block = pair_block.reshape(i_factors.shape[0], i_factors.shape[1], whole_rows.shape[0])
        swapped = lax.all_to_all(
            transpose_blocks(pair_block, blocks), "virt", split_axis=2, concat_axis=2, tiled=True
        )
        denominator = (
            virt_energy[None, :, None]
            + whole_energy[None, None, :]
            - occ_i[:, None, None]
            - occ_j[index]
        )
        amplitude = (swapped - 2.0 * pair_block) / denominator
        density = density + jnp.einsum(
            "iab,bp->iap", amplitude, whole_rows, precision=lax.Precision.HIGHEST
        )
    return density


def solution(mesh):
    placed = (
        P("conf", "virt", None),
        P("conf", "virt", None),
        P("conf"),
        P("conf"),
        P(("conf", "virt")),
    )
    return jax.shard_map(
        body, mesh=mesh, in_specs=placed, out_specs=P("conf", "virt", None), check_vma=False
    )
```

profile of v0, /device:TPU:16, one launch (start us, length us, event | category | flops | bytes accessed | tf_op | source)
XLA Modules:
  0.0 497.4 jit_solution(2721540128642686611)
XLA Ops:
  6.5 0.0 all-gather.7.cloned.1.call-start
  6.5 2.3 fusion.25
  8.8 0.0 all-gather.7.cloned.1.call-update
  8.8 0.0 all-gather.5.cloned.1.call-start
  8.9 0.7 all-gather.5.cloned.1.call-update
  9.6 74.7 %all-gather.7.cloned.1.call-done = f32[1,1024,2048]{2,1,0:T(8,128)} async-done(((f32[1,64,2048]{2,1,0:T(8,128)}), f32[1,1024,2048]{2,1,0:T(8,128)}) %all-gather.7.cloned.1.call-update) | async-done | bytes 8388624 | tf_op jit(solution)/shard_map/all_gather | solution.py:22
  84.3 33.7 %broadcast_multiply_fusion = (f32[1024,1024]{1,0:T(8,128)}, f32[1024,1024]{1,0:T(8,128)}) fusion(f32[1024,2048]{1,0:T(8,128)} %bitcast.40, f32[1,1024,2048]{2,1,0:T(8,128)} %all-gather.7.cloned.1.call-done), kind=kOutput, calls=%fused_computation.21 | convolution fusion | flops 25770852352 | bytes 25165824 | tf_op jit(solution)/shard_map/dot_general | solution.py:25
  118.0 7.3 %reshape_reshape.7 = f32[16,64,16,64]{3,2,1,0:T(8,128)} reshape(f32[1024,1024]{1,0:T(8,128)} %get-tuple-element.10) | data formatting | bytes 8388608 | tf_op jit(solution)/shard_map/reshape;reshape | solution.py:11
  125.3 11.5 %copy.16 = f32[16,64,16,64]{1,0,3,2:T(8,128)} copy(f32[16,64,16,64]{1,2,3,0:T(8,128)} %bitcast.36) | data formatting | bytes 8388608 | tf_op jit(solution)/shard_map/transpose | solution.py:12
  136.8 13.3 %reshape.60 = f32[16,1,65536]{2,1,0:T(1,128)} reshape(f32[1024,16,64]{2,1,0:T(8,128)} %bitcast.37) | data formatting | bytes 8388608
  150.1 5.9 %all-to-all-start.1 = ((f32[16,1,65536]{2,1,0:T(1,128)}), f32[16,1,65536]{2,1,0:T(1,128)}, u32[]{:S(2)}, u32[]{:S(2)}) async-start(f32[16,1,65536]{2,1,0:T(1,128)} %reshape.60), calls=%async_computation.1 | async-start | bytes 8388608 | tf_op jit(solution)/shard_map/all_to_all | solution.py:27
  156.0 3.4 all-gather.5.cloned.1.call-done
  159.4 33.7 %broadcast_multiply_fusion.1 = (f32[1024,1024]{1,0:T(8,128)}, f32[1024,1024]{1,0:T(8,128)}) fusion(f32[1024,2048]{1,0:T(8,128)} %bitcast.41, f32[1,1024,2048]{2,1,0:T(8,128)} %all-gather.5.cloned.1.call-done), kind=kOutput, calls=%fused_computation.22 | convolution fusion | flops 25770852352 | bytes 25165824 | tf_op jit(solution)/shard_map/dot_general | solution.py:25
  193.0 7.2 %reshape_reshape.6 = f32[16,64,16,64]{3,2,1,0:T(8,128)} reshape(f32[1024,1024]{1,0:T(8,128)} %get-tuple-element.12) | data formatting | bytes 8388608 | tf_op jit(solution)/shard_map/reshape;reshape | solution.py:11
  200.3 11.5 %copy.14 = f32[16,64,16,64]{1,0,3,2:T(8,128)} copy(f32[16,64,16,64]{1,2,3,0:T(8,128)} %bitcast.38) | data formatting | bytes 8388608 | tf_op jit(solution)/shard_map/transpose | solution.py:12
  211.7 13.3 %reshape.62 = f32[16,1,65536]{2,1,0:T(1,128)} reshape(f32[1024,16,64]{2,1,0:T(8,128)} %bitcast.39) | data formatting | bytes 8388608
  225.0 0.0 copy-start.5
  225.0 0.0 copy-start.2
  225.0 0.0 copy-start.1
  225.0 23.5 %all-to-all-done.1 = f32[16,1,65536]{2,1,0:T(1,128)} async-done(((f32[16,1,65536]{2,1,0:T(1,128)}), f32[16,1,65536]{2,1,0:T(1,128)}, u32[]{:S(2)}, u32[]{:S(2)}) %all-to-all-start.1) | async-done | bytes 4194336 | tf_op jit(solution)/shard_map/all_to_all | solution.py:27
  248.5 4.6 all-to-all-start
  253.1 0.0 copy-done.5
  253.1 0.6 dynamic-slice
  254.3 0.0 copy-done.2
  254.3 0.2 dynamic-update-slice
  254.6 109.4 %all-reduce = f32[1024]{0:T(1024)S(1)} all-reduce(f32[1024]{0:T(1024)S(1)} %dynamic-update-slice), channel_id=1, replica_groups=mesh['conf'=2,'virt'=16] {'virt'}, use_global_device_ids=true, to_apply=%add | all-reduce | flops 1024 | bytes 8192
  364.0 0.0 copy-done.1
  364.0 0.6 fusion.26
  364.6 0.1 broadcast_add_fusion
  364.7 0.6 broadcast.34
  365.3 13.7 %reduce = f32[16,65536]{1,0:T(8,128)} reduce(f32[16,1,65536]{2,1,0:T(1,128)} %all-to-all-done.1, f32[]{:T(128)} %broadcast.34), dimensions={1}, to_apply=%all_to_all.7.reduce_sub_computation | reduce | bytes 8388612 | tf_op jit(solution)/shard_map/all_to_all | solution.py:27
  379.0 6.9 %reshape.61 = f32[1024,16,64]{2,1,0:T(8,128)} reshape(f32[16,65536]{1,0:T(8,128)} %reduce) | data formatting | bytes 8388608
  386.0 6.8 %copy.17 = f32[16,64,1024]{2,1,0:T(8,128)} copy(f32[16,64,1024]{1,0,2:T(8,128)} %bitcast.34) | data formatting | bytes 8388608 | tf_op jit(solution)/shard_map/all_to_all | solution.py:27
  392.8 0.0 all-to-all-done
  392.8 13.8 %reduce.1 = f32[16,65536]{1,0:T(8,128)} reduce(f32[16,1,65536]{2,1,0:T(1,128)} %all-to-all-done, f32[]{:T(128)} %broadcast.34), dimensions={1}, to_apply=%all_to_all.6.reduce_sub_computation | reduce | bytes 8388612 | tf_op jit(solution)/shard_map/all_to_all | solution.py:27
  406.7 6.9 %reshape.63 = f32[1024,16,64]{2,1,0:T(8,128)} reshape(f32[16,65536]{1,0:T(8,128)} %reduce.1) | data formatting | bytes 8388608
  413.6 0.0 copy-start.3
  413.6 6.9 %copy.15 = f32[16,64,1024]{2,1,0:T(8,128)} copy(f32[16,64,1024]{1,0,2:T(8,128)} %bitcast.35) | data formatting | bytes 8388608 | tf_op jit(solution)/shard_map/all_to_all | solution.py:27
  420.5 0.0 copy-done.3
  420.5 0.0 copy-start
  420.5 0.0 copy-start.4
  420.5 33.6 %fusion = f32[16,64,2048]{2,1,0:T(8,128)S(1)} fusion(f32[1,1024,2048]{2,1,0:T(8,128)} %all-gather.7.cloned.1.call-done, f32[16,64,1024]{2,1,0:T(8,128)} %copy.17, f32[16,64,1024]{2,1,0:T(8,128)} %bitcast.42, f32[]{:T(128)} %bitcast.12, f32[16]{0:T(128)S(1)} %copy-done.3, f32[64,1024]{1,0:T(8,128)S(1)} %broadcast_add_fusion), kind=kOutput, calls=%fused_computation | convolution fusion | flops 25773998080 | bytes 25428036 | tf_op jit(solution)/shard_map/iab,bp->iap/dot_general | solution.py:37
  454.1 0.0 copy-done
  454.1 0.0 copy-done.4
  454.1 36.0 %fusion.14 = f32[16,64,2048]{2,1,0:T(8,128)} fusion(f32[16,64,2048]{2,1,0:T(8,128)S(1)} %fusion, f32[1,1024,2048]{2,1,0:T(8,128)} %all-gather.5.cloned.1.call-done, f32[16,64,1024]{2,1,0:T(8,128)S(1)} %copy-done, f32[16,64,1024]{2,1,0:T(8,128)S(1)} %bitcast.43, f32[]{:T(128)} %bitcast.6, f32[16]{0:T(128)S(1)} %copy-done.3, f32[64,1024]{1,0:T(8,128)S(1)} %broadcast_add_fusion), kind=kOutput, calls=%fused_computation.14 | convolution fusion | flops 25776095232 | bytes 33816644 | tf_op jit(solution)/shard_map/iab,bp->iap/dot_general | solution.py:37
  (1 shorter events, 0.0 us)
Async XLA Ops:
  6.5 77.8 %all-gather.7.cloned.1.call-start = ((), (), s32[]{:S(2)}) async-start(), calls=%async_computation.3 | async-start | bytes 8912896 | tf_op jit(solution)/shard_map/all_gather | solution.py:22
  8.8 150.6 %all-gather.5.cloned.1.call-start = ((), (), s32[]{:S(2)}) async-start(), calls=%async_computation.2 | async-start | bytes 8912896 | tf_op jit(solution)/shard_map/all_gather | solution.py:22
  150.1 98.4 %all-to-all-start.1 = ((f32[16,1,65536]{2,1,0:T(1,128)}), f32[16,1,65536]{2,1,0:T(1,128)}, u32[]{:S(2)}, u32[]{:S(2)}) async-start(f32[16,1,65536]{2,1,0:T(1,128)} %reshape.60), calls=%async_computation.1 | async-start | bytes 8388608 | tf_op jit(solution)/shard_map/all_to_all | solution.py:27
  225.0 28.1 %copy-start.5 = (u32[32]{0:T(128)S(1)}, u32[32]{0:T(128)}, u32[]{:S(2)}) copy-start(u32[32]{0:T(128)} %constant.4) | copy-start | bytes 388
  225.0 29.3 %copy-start.2 = (f32[64]{0:T(128)S(1)}, f32[64]{0:T(128)}, u32[]{:S(2)}) copy-start(f32[64]{0:T(128)} %param.9) | copy-start | bytes 772
  225.0 139.0 %copy-start.1 = (f32[2]{0:T(128)S(1)}, f32[2]{0:T(128)}, u32[]{:S(2)}) copy-start(f32[2]{0:T(128)} %param.8) | copy-start | bytes 28
  248.5 144.3 %all-to-all-start = ((f32[16,1,65536]{2,1,0:T(1,128)}), f32[16,1,65536]{2,1,0:T(1,128)}, u32[]{:S(2)}, u32[]{:S(2)}) async-start(f32[16,1,65536]{2,1,0:T(1,128)} %reshape.62), calls=%async_computation | async-start | bytes 8388608 | tf_op jit(solution)/shard_map/all_to_all | solution.py:27
  413.6 6.9 %copy-start.3 = (f32[16]{0:T(128)S(1)}, f32[16]{0:T(128)}, u32[]{:S(2)}) copy-start(f32[16]{0:T(128)} %param.7) | copy-start | bytes 196
  420.5 33.6 %copy-start = (f32[16,64,1024]{2,1,0:T(8,128)S(1)}, f32[16,64,1024]{2,1,0:T(8,128)}, u32[]{:S(2)}) copy-start(f32[16,64,1024]{2,1,0:T(8,128)} %copy.15) | copy-start | bytes 12582916
  420.5 33.6 %copy-start.4 = (f32[1024,1024]{1,0:T(8,128)S(1)}, f32[1024,1024]{1,0:T(8,128)}, u32[]{:S(2)}) copy-start(f32[1024,1024]{1,0:T(8,128)} %get-tuple-element.11) | copy-start | bytes 12582916
Sparse Core Ops, SparseCore 0:
  9.5 74.7 all-gather.6
  86.5 72.8 all-gather.4
where the time goes:
time: 507 us; the launch traced here: 497 us
  matrix products  137 us (27%)
  blocking collectives  109 us (21%)
  waiting for transfers between devices  102 us (20%)
  local copies, waits for them, and re-layouts  95.9 us (19%)
  other arithmetic  27.6 us (5%)
  between operations  14.6 us (3%)
  starting transfers between devices  10.5 us (2%)
    unnamed x1, blocking collectives  109 us
    all_gather x2, waiting for transfers between devices, body(): lax.all_gather(j_factors[index], 'virt', axis=0, tiled=True)  78.1 us
    dot_general x2, matrix products, body(): jnp.einsum('iab,bp->iap', amplitude, whole_rows, precision=lax.Precision....  69.6 us
    dot_general x2, matrix products, body(): jnp.dot(left_rows, whole_rows.T, precision=lax.Precision.HIGHEST)  67.4 us
    unnamed x19, local copies, waits for them, and re-layouts  41.3 us
    all_to_all x2, other arithmetic, body(): lax.all_to_all(transpose_blocks(pair_block, blocks), 'virt', split_axis=2...  27.6 us
    all_to_all x2, waiting for transfers between devices, body(): lax.all_to_all(transpose_blocks(pair_block, blocks), 'virt', split_axis=2...  23.5 us
    transpose x2, local copies, waits for them, and re-layouts, transpose_blocks(): moved = jnp.swapaxes(split, -1, -3)  22.9 us
  transfers between devices with their start and end apart: 4, of which 3 were waited for; matrix products, arithmetic and copies ran while one was open for 32% of the time, Pallas kernels for 0%

commit v1 on v0

v1 whole, which is shorter than its diff:
```python
import functools

import jax
import jax.numpy as jnp
from jax import lax
from jax.experimental import pallas as pl
from jax.experimental.pallas import tpu as pltpu
from jax.sharding import PartitionSpec as P

LANES = 128
MESH = pl.DeviceIdType.MESH


def split(value):
    high = value.astype(jnp.bfloat16)
    low = (value - high.astype(jnp.float32)).astype(jnp.bfloat16)
    return high, low


def kernel(
    n, columns, i_ref, j_ref, row_ref, col_ref, out_ref,
    i_high, i_low, j_all, direct, x_send, x_recv, total, j_parts, amp_parts,
    local_sem, j_send_sem, j_recv_sem, x_send_sem, x_recv_sem,
):
    levels = n // 2 // columns
    me = lax.axis_index("virt")
    core = lax.rem(me, 2)
    chip = me // 2
    y = lax.rem(chip, columns)
    z = chip // columns
    rows, depth = i_ref.shape
    pair = 2 * LANES
    tall = 256
    wide = 512

    load_i = pltpu.make_async_copy(i_ref, total, local_sem.at[0])
    load_i.start()
    load_j = pltpu.make_async_copy(j_ref, j_all.at[me], local_sem.at[1])
    load_j.start()

    barrier = pltpu.get_barrier_semaphore()

    @pl.loop(1, n)
    def _(step):
        pl.semaphore_signal(
            barrier, inc=1, device_id={"virt": lax.rem(me + step, n)}, device_id_type=MESH
        )

    pl.semaphore_wait(barrier, n - 1)

    def j_copy(origin, way, device):
        return pltpu.make_async_remote_copy(
            src_ref=j_all.at[origin],
            dst_ref=j_all.at[origin],
            send_sem=j_send_sem.at[origin, way],
            recv_sem=j_recv_sem.at[origin],
            device_id={"virt": device},
            device_id_type=MESH,
        )

    def j_targets(origin, act):
        place = origin // 2
        same_core = lax.rem(origin, 2) == core
        in_column = jnp.logical_and(same_core, lax.rem(place, columns) == y)
        from_z = place // columns

        @pl.when(jnp.logical_and(in_column, jnp.logical_and(z >= from_z, z + 1 < levels)))
        def _():
            act(j_copy(origin, 0, me + 2 * columns))

        @pl.when(jnp.logical_and(in_column, jnp.logical_and(z <= from_z, z > 0)))
        def _():
            act(j_copy(origin, 1, me - 2 * columns))

        if columns == 2:
            @pl.when(in_column)
            def _():
                act(j_copy(origin, 2, me + 2 * (1 - 2 * y)))

        @pl.when(same_core)
        def _():
            act(j_copy(origin, 3, me + 1 - 2 * core))

    def x_copy(other):
        return pltpu.make_async_remote_copy(
            src_ref=x_send.at[other],
            dst_ref=x_recv.at[me],
            send_sem=x_send_sem.at[other],
            recv_sem=x_recv_sem.at[me],
            device_id={"virt": other},
            device_id_type=MESH,
        )

    def x_arrival(other):
        return pltpu.make_async_remote_copy(
            src_ref=x_send.at[other],
            dst_ref=x_recv.at[other],
            send_sem=x_send_sem.at[other],
            recv_sem=x_recv_sem.at[other],
            device_id={"virt": other},
            device_id_type=MESH,
        )

    def x_stay():
        return pltpu.make_async_copy(x_send.at[me], x_recv.at[me], local_sem.at[2])

    load_j.wait()
    j_targets(me, lambda copy: copy.start())
    load_i.wait()

    @pl.loop(0, rows // 32)
    def _(step):
        part = pl.ds(pl.multiple_of(step * 32, 32), 32)
        high, low = split(total[part, :])
        i_high[part, :] = high
        i_low[part, :] = low
        total[part, :] = jnp.zeros((32, depth), jnp.float32)

    @pl.loop(0, n)
    def _(other):
        x_send[other, pl.ds(rows, 8), :] = col_ref[...]

    def split_j(place, copies):
        per = LANES // 32

        @pl.loop(0, 2 * per)
        def _(step):
            from_rows = pl.ds(pl.multiple_of(lax.rem(step, per) * 32, 32), 32)
            high, low = split(j_all[2 * place + step // per, from_rows, :])
            base = pl.multiple_of(step * 32, 32)
            j_parts[pl.ds(base, 32), :] = high
            j_parts[pl.ds(pair + base, 32), :] = low
            if copies == 3:
                j_parts[pl.ds(2 * pair + base, 32), :] = high

    def visit(step):
        level = step // 4
        kind = lax.rem(step // 2, 2)
        sign = lax.rem(step, 2)
        distance = level - kind
        at_y = jnp.where(kind == 0, y, columns - 1 - y)

        def on(way):
            at_z = z + (1 - 2 * way) * distance
            valid = jnp.logical_and(distance >= 0, jnp.logical_and(at_z >= 0, at_z < levels))
            valid = jnp.logical_and(valid, jnp.logical_or(distance > 0, way == 0))
            if columns == 1:
                valid = jnp.logical_and(valid, kind == 0)
            return valid, at_z * columns + at_y

        return on, sign

    visits = 4 * (levels + columns - 1)

    @pl.loop(0, visits)
    def _(step):
        on, sign = visit(step)

        @pl.when(sign == 0)
        def _():
            for way in range(2):
                valid, place = on(way)
                origin = 2 * place + core

                @pl.when(jnp.logical_and(valid, origin != me))
                def _():
                    j_copy(origin, 0, me).wait_recv()
                    j_targets(origin, lambda copy: copy.start())

        valid, place = on(sign)

        @pl.when(valid)
        def _():
            j_copy(2 * place + 1 - core, 0, me).wait_recv()
            split_j(place, 2)
            lane = lax.broadcasted_iota(jnp.int32, (LANES // 2, LANES), 1)
            half = LANES // 2
            contract = (((1,), (1,)), ((), ()))

            @pl.loop(0, rows // tall)
            def _(block):
                start = pl.multiple_of(block * tall, tall)
                high, low = i_high[pl.ds(start, tall), :], i_low[pl.ds(start, tall), :]
                j_high, j_low = j_parts[pl.ds(0, pair), :], j_parts[pl.ds(pair, pair), :]
                dot = functools.partial(
                    lax.dot_general, dimension_numbers=contract,
                    preferred_element_type=jnp.float32,
                )
                block_pair = dot(high, j_high) + (dot(high, j_low) + dot(low, j_high))
                direct[place, pl.ds(start, tall), :] = block_pair
                for side in range(2):
                    for group in range(tall // LANES):
                        tile = block_pair[
                            group * LANES:(group + 1) * LANES, side * LANES:(side + 1) * LANES
                        ]
                        turned = tile.T
                        moved = pltpu.roll(turned, half, 1)
                        first = jnp.where(lane < half, turned[:half], moved[half:])
                        second = jnp.where(lane < half, moved[:half], turned[half:])
                        base = start + group * LANES
                        x_send[2 * place + side, pl.ds(base, half), :] = first
                        x_send[2 * place + side, pl.ds(base + half, half), :] = second

            for side in range(2):
                other = 2 * place + side

                @pl.when(other != me)
                def _():
                    x_copy(other).start()

                @pl.when(other == me)
                def _():
                    x_stay().start()

    @pl.loop(0, visits)
    def _(step):
        on, sign = visit(step)
        valid, place = on(sign)

        @pl.when(valid)
        def _():
            split_j(place, 3)
            for side in range(2):
                other = 2 * place + side

                @pl.when(other != me)
                def _():
                    x_arrival(other).wait_recv()

                @pl.when(other == me)
                def _():
                    x_stay().wait()

            @pl.loop(0, rows // tall)
            def _(block):
                part = pl.ds(pl.multiple_of(block * tall, tall), tall)
                for side in range(2):
                    other = 2 * place + side
                    lanes = slice(side * LANES, (side + 1) * LANES)
                    swapped = x_recv[other, part, :]
                    own = direct[place, part, lanes]
                    denominator = row_ref[part, :] + x_recv[other, pl.ds(rows, 8), :][0:1]
                    high, low = split((swapped - 2.0 * own) / denominator)
                    amp_parts[:, side * LANES:(side + 1) * LANES] = high
                    amp_parts[:, pair + side * LANES:pair + (side + 1) * LANES] = high
                    amp_parts[:, 2 * pair + side * LANES:2 * pair + (side + 1) * LANES] = low

                @pl.loop(0, depth // wide)
                def _(strip):
                    at = pl.ds(pl.multiple_of(strip * wide, wide), wide)
                    total[part, at] += jnp.dot(
                        amp_parts[...], j_parts[:, at], preferred_element_type=jnp.float32
                    )

    store = pltpu.make_async_copy(total, out_ref, local_sem.at[0])
    store.start()

    @pl.loop(0, n)
    def _(other):
        j_targets(other, lambda copy: copy.wait_send())

        @pl.when(other != me)
        def _():
            x_copy(other).wait_send()

    store.wait()


def fused(columns, i_factors, j_factors, occ_i, occ_j, virt_energy):
    n = lax.axis_size("virt")
    ni, width, depth = i_factors.shape
    nj = j_factors.shape[0]
    rows = ni * width
    row_term = (virt_energy[None, :] - occ_i[:, None]).reshape(rows, 1)
    row_term = jnp.broadcast_to(row_term, (rows, LANES))
    col_term = (virt_energy[None, :] - occ_j[:, None]).reshape(1, nj * width)
    col_term = jnp.broadcast_to(col_term, (8, LANES))
    anywhere = pl.BlockSpec(memory_space=pl.ANY)
    vmem = pl.BlockSpec(memory_space=pltpu.VMEM)
    f32, bf16 = jnp.float32, jnp.bfloat16
    dma = pltpu.SemaphoreType.DMA
    out = pl.pallas_call(
        functools.partial(kernel, n, columns),
        out_shape=jax.ShapeDtypeStruct((rows, depth), f32),
        in_specs=[anywhere, anywhere, vmem, vmem],
        out_specs=anywhere,
        scratch_shapes=[
            pltpu.VMEM((rows, depth), bf16),
            pltpu.VMEM((rows, depth), bf16),
            pltpu.VMEM((n, LANES, depth), f32),
            pltpu.VMEM((n // 2, rows, 2 * LANES), f32),
            pltpu.VMEM((n, rows + 8, LANES), f32),
            pltpu.VMEM((n, rows + 8, LANES), f32),
            pltpu.VMEM((rows, depth), f32),
            pltpu.VMEM((6 * LANES, depth), bf16),
            pltpu.VMEM((256, 6 * LANES), bf16),
            dma((3,)),
            dma((n, 4)),
            dma((n,)),
            dma((n,)),
            dma((n,)),
        ],
        compiler_params=pltpu.CompilerParams(
            collective_id=0, has_side_effects=True, vmem_limit_bytes=67043328
        ),
        name="pair_exchange",
    )(i_factors.reshape(rows, depth), j_factors.reshape(nj * width, depth), row_term, col_term)
    return out.reshape(i_factors.shape)


def transpose_blocks(pair_block, blocks):
    leading = pair_block.shape[:-2]
    height = pair_block.shape[-2]
    width = pair_block.shape[-1]
    parts = pair_block.reshape(leading + (height, blocks, height))
    moved = jnp.swapaxes(parts, -1, -3)
    return moved.reshape(leading + (height, width))


def general(i_factors, j_factors, occ_i, occ_j, virt_energy):
    blocks = lax.axis_size("virt")
    left_rows = i_factors.reshape(-1, i_factors.shape[2])
    density = jnp.zeros(i_factors.shape, jnp.float32)
    whole_energy = lax.all_gather(virt_energy, "virt", axis=0, tiled=True)
    for index in range(j_factors.shape[0]):
        whole_rows = lax.all_gather(j_factors[index], "virt", axis=0, tiled=True)
        pair_block = jnp.dot(left_rows, whole_rows.T, precision=lax.Precision.HIGHEST)
        pair_block = pair_block.reshape(i_factors.shape[0], i_factors.shape[1], whole_rows.shape[0])
        swapped = lax.all_to_all(
            transpose_blocks(pair_block, blocks), "virt", split_axis=2, concat_axis=2, tiled=True
        )
        denominator = (
            virt_energy[None, :, None]
            + whole_energy[None, None, :]
            - occ_i[:, None, None]
            - occ_j[index]
        )
        amplitude = (swapped - 2.0 * pair_block) / denominator
        density = density + jnp.einsum(
            "iab,bp->iap", amplitude, whole_rows, precision=lax.Precision.HIGHEST
        )
    return density


def chip_columns(mesh):
    group = list(mesh.devices.reshape(-1, mesh.shape["virt"])[0])
    if len(group) % 2:
        return 0
    chips = group[::2]
    heights = len({getattr(device, "coords", (0, 0, place))[2] for place, device in enumerate(chips)})
    columns, left = divmod(len(chips), heights)
    return columns if left == 0 and columns in (1, 2) else 0


def body(columns, i_factors, j_factors, occ_i, occ_j, virt_energy):
    ni, width, depth = i_factors.shape
    nj = j_factors.shape[0]
    fits = nj == 2 and nj * width == LANES and (ni * width) % 256 == 0 and depth % 512 == 0
    n = lax.axis_size("virt")
    room = 4 * ni * width * depth * 2 + 4 * n * LANES * (depth + 3 * (ni * width + 8))
    if columns and fits and room < 58 * 2**20:
        return fused(columns, i_factors, j_factors, occ_i, occ_j, virt_energy)
    return general(i_factors, j_factors, occ_i, occ_j, virt_energy)


def solution(mesh):
    placed = (
        P("conf", "virt", None),
        P("conf", "virt", None),
        P("conf"),
        P("conf"),
        P(("conf", "virt")),
    )
    return jax.shard_map(
        functools.partial(body, chip_columns(mesh)),
        mesh=mesh, in_specs=placed, out_specs=P("conf", "virt", None), check_vma=False,
    )
```

time: 507 us -> 267 us (0.53)
  the two profiles are of different devices: /device:TPU:16 before, /device:TPU:1 now
where the time goes in v1:
time: 267 us; the launch traced here: 266 us
  Pallas kernels  255 us (96%)
  local copies, waits for them, and re-layouts  9.63 us (4%)
    pallas_call x1, Pallas kernels, fused(): pl.pallas_call(functools.partial(kernel, n, columns), out_shape=jax.Shape...  255 us
    unnamed x1, local copies, waits for them, and re-layouts  7.89 us

profile of v1, /device:TPU:1, one launch (start us, length us, event | category | flops | bytes accessed | tf_op | source)
XLA Modules:
  0.0 266.4 jit_solution(1716899361114830335)
XLA Ops:
  0.0 0.7 broadcast_subtract_fusion.1
  0.7 0.1 sub.47
  0.8 0.6 broadcast_in_dim.5.col_ref
  1.4 0.7 broadcast_subtract_fusion
  2.2 0.1 sub.43
  2.2 1.0 broadcast_in_dim.4.row_ref
  3.2 255.2 %pair_exchange.1 = f32[1024,2048]{1,0:T(8,128)} custom-call(f32[1024,2048]{1,0:T(8,128)} %bitcast.4, f32[128,2048]{1,0:T(8,128)} %bitcast.5, f32[1024,128]{1,0:T(8,128)} %broadcast_in_dim.4.row_ref, f32[8,128]{1,0:T(8,128)} %broadcast_in_dim.5.col_ref), custom_call_target="tpu_custom_call" | custom-call | tf_op jit(solution)/shard_map/pair_exchange/pallas_call | solution.py:282
  258.5 7.9 %copy.7 = f32[16,64,2048]{2,1,0:T(8,128)} copy(f32[16,64,2048]{2,1,0:T(8,128)} %bitcast.3) | data formatting | bytes 16777216

commit v2 on v1

--- a/solution.py
+++ b/solution.py
@@ -18,9 +18,9 @@
 
 
 def kernel(
-    n, columns, i_ref, j_ref, row_ref, col_ref, out_ref,
-    i_high, i_low, j_all, direct, x_send, x_recv, total, j_parts, amp_parts,
-    local_sem, j_send_sem, j_recv_sem, x_send_sem, x_recv_sem,
+    n, columns, i_ref, j_ref, energy_ref, occ_i_ref, occ_j_ref, part_ref, amp_ref, last_j_ref,
+    i_high, i_low, j_all, direct, x_send, x_recv, total, j_parts, amp_parts, row_ref,
+    local_sem, j_send_sem, j_recv_sem, x_send_sem, x_recv_sem, amp_sem,
 ):
     levels = n // 2 // columns
     me = lax.axis_index("virt")
@@ -83,8 +83,8 @@
 
     def x_copy(other):
         return pltpu.make_async_remote_copy(
-            src_ref=x_send.at[other],
-            dst_ref=x_recv.at[me],
+            src_ref=x_send.at[other, pl.ds(0, rows + 1)],
+            dst_ref=x_recv.at[me, pl.ds(0, rows + 1)],
             send_sem=x_send_sem.at[other],
             recv_sem=x_recv_sem.at[me],
             device_id={"virt": other},
@@ -93,8 +93,8 @@
 
     def x_arrival(other):
         return pltpu.make_async_remote_copy(
-            src_ref=x_send.at[other],
-            dst_ref=x_recv.at[other],
+            src_ref=x_send.at[other, pl.ds(0, rows + 1)],
+            dst_ref=x_recv.at[other, pl.ds(0, rows + 1)],
             send_sem=x_send_sem.at[other],
             recv_sem=x_recv_sem.at[other],
             device_id={"virt": other},
@@ -116,9 +116,20 @@
         i_low[part, :] = low
         total[part, :] = jnp.zeros((32, depth), jnp.float32)
 
+    width = energy_ref.shape[1]
+    energy = energy_ref[...]
+    twice = jnp.concatenate([energy, energy], axis=1)
+    tall_energy = jnp.broadcast_to(twice, (LANES, LANES)).T[:width]
+    for orbital in range(rows // width):
+        row_ref[orbital * width:(orbital + 1) * width, :] = tall_energy - occ_i_ref[orbital]
+    col_lane = lax.broadcasted_iota(jnp.int32, (8, LANES), 1)
+    col_term = jnp.broadcast_to(twice, (8, LANES)) - jnp.where(
+        col_lane < width, occ_j_ref[0], occ_j_ref[1]
+    )
+
     @pl.loop(0, n)
     def _(other):
-        x_send[other, pl.ds(rows, 8), :] = col_ref[...]
+        x_send[other, pl.ds(rows, 8), :] = col_term
 
     def split_j(place, copies):
         per = LANES // 32
@@ -133,6 +144,8 @@
             if copies == 3:
                 j_parts[pl.ds(2 * pair + base, 32), :] = high
 
+    toward = jnp.where(2 * z >= levels, -1, 1)
+
     def visit(step):
         level = step // 4
         kind = lax.rem(step // 2, 2)
@@ -141,7 +154,7 @@
         at_y = jnp.where(kind == 0, y, columns - 1 - y)
 
         def on(way):
-            at_z = z + (1 - 2 * way) * distance
+            at_z = z + toward * (1 - 2 * way) * distance
             valid = jnp.logical_and(distance >= 0, jnp.logical_and(at_z >= 0, at_z < levels))
             valid = jnp.logical_and(valid, jnp.logical_or(distance > 0, way == 0))
             if columns == 1:
@@ -212,58 +225,100 @@
                 def _():
                     x_stay().start()
 
+    def await_blocks(place):
+        for side in range(2):
+            other = 2 * place + side
+
+            @pl.when(other != me)
+            def _():
+                x_arrival(other).wait_recv()
+
+            @pl.when(other == me)
+            def _():
+                x_stay().wait()
+
+    def amplitudes(place, part):
+        for side in range(2):
+            other = 2 * place + side
+            lanes = slice(side * LANES, (side + 1) * LANES)
+            swapped = x_recv[other, part, :]
+            own = direct[place, part, lanes]
+            denominator = row_ref[part, :] + x_recv[other, pl.ds(rows, 1), :]
+            high, low = split((swapped - 2.0 * own) / denominator)
+            amp_parts[part, side * LANES:(side + 1) * LANES] = high
+            amp_parts[part, pair + side * LANES:pair + (side + 1) * LANES] = high
+            amp_parts[part, 2 * pair + side * LANES:2 * pair + (side + 1) * LANES] = low
+
+    farthest = jnp.maximum(z, levels - 1 - z)
+    back = z - toward * farthest
+    forth = z + toward * farthest
+    back_valid = jnp.logical_and(back >= 0, back < levels)
+    last_place = jnp.where(back_valid, back, forth) * columns + columns - 1 - y
+
     @pl.loop(0, visits)
     def _(step):
         on, sign = visit(step)
         valid, place = on(sign)
 
-        @pl.when(valid)
+        @pl.when(jnp.logical_and(valid, place != last_place))
         def _():
             split_j(place, 3)
-            for side in range(2):
-                other = 2 * place + side
-
-                @pl.when(other != me)
-                def _():
-                    x_arrival(other).wait_recv()
-
-                @pl.when(other == me)
-                def _():
-                    x_stay().wait()
+            await_blocks(place)
 
             @pl.loop(0, rows // tall)
             def _(block):
                 part = pl.ds(pl.multiple_of(block * tall, tall), tall)
-                for side in range(2):
-                    other = 2 * place + side
-                    lanes = slice(side * LANES, (side + 1) * LANES)
-                    swapped = x_recv[other, part, :]
-                    own = direct[place, part, lanes]
-                    denominator = row_ref[part, :] + x_recv[other, pl.ds(rows, 8), :][0:1]
-                    high, low = split((swapped - 2.0 * own) / denominator)
-                    amp_parts[:, side * LANES:(side + 1) * LANES] = high
-                    amp_parts[:, pair + side * LANES:pair + (side + 1) * LANES] = high
-                    amp_parts[:, 2 * pair + side * LANES:2 * pair + (side + 1) * LANES] = low
+                amplitudes(place, part)
 
                 @pl.loop(0, depth // wide)
                 def _(strip):
                     at = pl.ds(pl.multiple_of(strip * wide, wide), wide)
                     total[part, at] += jnp.dot(
-                        amp_parts[...], j_parts[:, at], preferred_element_type=jnp.float32
+                        amp_parts[part, :], j_parts[:, at], preferred_element_type=jnp.float32
                     )
 
-    store = pltpu.make_async_copy(total, out_ref, local_sem.at[0])
+    store = pltpu.make_async_copy(total, part_ref, local_sem.at[0])
     store.start()
+    split_j(last_place, 3)
+    store_j = pltpu.make_async_copy(j_parts, last_j_ref, local_sem.at[1])
+    store_j.start()
 
     @pl.loop(0, n)
     def _(other):
         j_targets(other, lambda copy: copy.wait_send())
 
+    await_blocks(last_place)
+
+    def store_amp(block):
+        part = pl.ds(pl.multiple_of(block * tall, tall), tall)
+        return pltpu.make_async_copy(amp_parts.at[part], amp_ref.at[part], amp_sem.at[block])
+
+    @pl.loop(0, rows // tall)
+    def _(block):
+        amplitudes(last_place, pl.ds(pl.multiple_of(block * tall, tall), tall))
+        store_amp(block).start()
+
+    @pl.loop(0, n)
+    def _(other):
         @pl.when(other != me)
         def _():
             x_copy(other).wait_send()
 
     store.wait()
+    store_j.wait()
+
+    @pl.loop(0, rows // tall)
+    def _(block):
+        store_amp(block).wait()
+
+
+def finish(part_ref, amp_ref, j_ref, out_ref):
+    wide = 512
+    for start in range(0, part_ref.shape[1], wide):
+        at = slice(start, start + wide)
+        out_ref[:, at] = part_ref[:, at] + jnp.dot(
+            amp_ref[...], j_ref[:, at], preferred_element_type=jnp.float32
+        )
 
 
 def fused(columns, i_factors, j_factors, occ_i, occ_j, virt_energy):
@@ -271,19 +326,20 @@
     ni, width, depth = i_factors.shape
     nj = j_factors.shape[0]
     rows = ni * width
-    row_term = (virt_energy[None, :] - occ_i[:, None]).reshape(rows, 1)
-    row_term = jnp.broadcast_to(row_term, (rows, LANES))
-    col_term = (virt_energy[None, :] - occ_j[:, None]).reshape(1, nj * width)
-    col_term = jnp.broadcast_to(col_term, (8, LANES))
     anywhere = pl.BlockSpec(memory_space=pl.ANY)
     vmem = pl.BlockSpec(memory_space=pltpu.VMEM)
     f32, bf16 = jnp.float32, jnp.bfloat16
     dma = pltpu.SemaphoreType.DMA
-    out = pl.pallas_call(
+    smem = pl.BlockSpec(memory_space=pltpu.SMEM)
+    part, amp, last_j = pl.pallas_call(
         functools.partial(kernel, n, columns),
-        out_shape=jax.ShapeDtypeStruct((rows, depth), f32),
-        in_specs=[anywhere, anywhere, vmem, vmem],
-        out_specs=anywhere,
+        out_shape=(
+            jax.ShapeDtypeStruct((rows, depth), f32),
+            jax.ShapeDtypeStruct((rows, 6 * LANES), bf16),
+            jax.ShapeDtypeStruct((6 * LANES, depth), bf16),
+        ),
+        in_specs=[anywhere, anywhere, vmem, smem, smem],
+        out_specs=(anywhere, anywhere, anywhere),
         scratch_shapes=[
             pltpu.VMEM((rows, depth), bf16),
             pltpu.VMEM((rows, depth), bf16),
@@ -293,18 +349,36 @@
             pltpu.VMEM((n, rows + 8, LANES), f32),
             pltpu.VMEM((rows, depth), f32),
             pltpu.VMEM((6 * LANES, depth), bf16),
-            pltpu.VMEM((256, 6 * LANES), bf16),
+            pltpu.VMEM((rows, 6 * LANES), bf16),
+            pltpu.VMEM((rows, LANES), f32),
             dma((3,)),
             dma((n, 4)),
             dma((n,)),
             dma((n,)),
             dma((n,)),
+            dma((rows // 256,)),
         ],
         compiler_params=pltpu.CompilerParams(
             collective_id=0, has_side_effects=True, vmem_limit_bytes=67043328
         ),
         name="pair_exchange",
-    )(i_factors.reshape(rows, depth), j_factors.reshape(nj * width, depth), row_term, col_term)
+    )(
+        i_factors.reshape(rows, depth), j_factors.reshape(nj * width, depth),
+        virt_energy.reshape(1, width), occ_i, occ_j,
+    )
+    tall = 128
+    out = pl.pallas_call(
+        finish,
+        out_shape=jax.ShapeDtypeStruct((rows, depth), f32),
+        grid=(rows // tall,),
+        in_specs=[
+            pl.BlockSpec((tall, depth), lambda step: (step, 0)),
+            pl.BlockSpec((tall, 6 * LANES), lambda step: (step, 0)),
+            pl.BlockSpec((6 * LANES, depth), lambda step: (0, 0)),
+        ],
+        out_specs=pl.BlockSpec((tall, depth), lambda step: (step, 0)),
+        name="last_block",
+    )(part, amp, last_j)
     return out.reshape(i_factors.shape)
 
 

time: 267 us -> 261 us (0.978)
  local copies, waits for them, and re-layouts: 9.63 us -> 0 us
  Pallas kernels: 255 us -> 261 us
    unnamed x1 -> x0, local copies, waits for them, and re-layouts: 7.89 us -> none
    pallas_call x1 -> x2, Pallas kernels: 255 us -> 261 us  [the longest x1 248 us: fused(): pl.pallas_call(functools.partial(kernel, n, columns), out_shape=(jax.Shap...]
where the time goes in v2:
time: 261 us
  Pallas kernels  261 us (100%)
    pallas_call x1, Pallas kernels, fused(): pl.pallas_call(functools.partial(kernel, n, columns), out_shape=(jax.Shap...  248 us
    pallas_call x1, Pallas kernels, fused(): pl.pallas_call(finish, out_shape=jax.ShapeDtypeStruct((rows, depth), f32)...  12.1 us

profile of v2, /device:TPU:1, one launch (start us, length us, event | category | flops | bytes accessed | tf_op | source)
XLA Modules:
  0.0 260.5 jit_solution(17500662884597636019)
XLA Ops:
  0.0 248.4 %pair_exchange.1 = (f32[1024,2048]{1,0:T(8,128)}, bf16[1024,768]{1,0:T(8,128)(2,1)}, bf16[768,2048]{1,0:T(8,128)(2,1)}) custom-call(f32[1024,2048]{1,0:T(8,128)} %bitcast.4, f32[128,2048]{1,0:T(8,128)} %bitcast.5, f32[1,64]{1,0:T(1,128)} %bitcast.6, f32[16]{0:T(128)} %occ_i_ref.1, f32[2]{0:T(128)} %occ_j_ref.1), custom_call_target="tpu_custom_call" | custom-call | tf_op jit(solution)/shard_map/pair_exchange/pallas_call | solution.py:334
  248.4 12.1 %last_block.1 = f32[1024,2048]{1,0:T(8,128)} custom-call(f32[1024,2048]{1,0:T(8,128)} %get-tuple-element.8.part_ref, bf16[1024,768]{1,0:T(8,128)(2,1)} %get-tuple-element.9.amp_ref, bf16[768,2048]{1,0:T(8,128)(2,1)} %get-tuple-element.10.j_ref), custom_call_target="tpu_custom_call" | custom-call | tf_op jit(solution)/shard_map/last_block/pallas_call | solution.py:370

commit v3 on v2

--- a/solution.py
+++ b/solution.py
@@ -267,15 +267,14 @@
 
             @pl.loop(0, rows // tall)
             def _(block):
-                part = pl.ds(pl.multiple_of(block * tall, tall), tall)
-                amplitudes(place, part)
-
-                @pl.loop(0, depth // wide)
-                def _(strip):
-                    at = pl.ds(pl.multiple_of(strip * wide, wide), wide)
-                    total[part, at] += jnp.dot(
-                        amp_parts[part, :], j_parts[:, at], preferred_element_type=jnp.float32
-                    )
+                amplitudes(place, pl.ds(pl.multiple_of(block * tall, tall), tall))
+
+            @pl.loop(0, depth // pair)
+            def _(strip):
+                at = pl.ds(pl.multiple_of(strip * pair, pair), pair)
+                total[:, at] += jnp.dot(
+                    amp_parts[...], j_parts[:, at], preferred_element_type=jnp.float32
+                )
 
     store = pltpu.make_async_copy(total, part_ref, local_sem.at[0])
     store.start()
@@ -313,7 +312,7 @@
 
 
 def finish(part_ref, amp_ref, j_ref, out_ref):
-    wide = 512
+    wide = 256
     for start in range(0, part_ref.shape[1], wide):
         at = slice(start, start + wide)
         out_ref[:, at] = part_ref[:, at] + jnp.dot(
@@ -366,7 +365,7 @@
         i_factors.reshape(rows, depth), j_factors.reshape(nj * width, depth),
         virt_energy.reshape(1, width), occ_i, occ_j,
     )
-    tall = 128
+    tall = 256
     out = pl.pallas_call(
         finish,
         out_shape=jax.ShapeDtypeStruct((rows, depth), f32),

time: 261 us -> 257 us (0.985)
  Pallas kernels: 261 us -> 257 us
where the time goes in v3:
time: 257 us
  Pallas kernels  257 us (100%)
    pallas_call x1, Pallas kernels, fused(): pl.pallas_call(functools.partial(kernel, n, columns), out_shape=(jax.Shap...  247 us
    pallas_call x1, Pallas kernels, fused(): pl.pallas_call(finish, out_shape=jax.ShapeDtypeStruct((rows, depth), f32)...  10.1 us

profile of v3, /device:TPU:1, one launch (start us, length us, event | category | flops | bytes accessed | tf_op | source)
XLA Modules:
  0.0 257.3 jit_solution(16096290307146614693)
XLA Ops:
  0.0 247.2 %pair_exchange.1 = (f32[1024,2048]{1,0:T(8,128)}, bf16[1024,768]{1,0:T(8,128)(2,1)}, bf16[768,2048]{1,0:T(8,128)(2,1)}) custom-call(f32[1024,2048]{1,0:T(8,128)} %bitcast.4, f32[128,2048]{1,0:T(8,128)} %bitcast.5, f32[1,64]{1,0:T(1,128)} %bitcast.6, f32[16]{0:T(128)} %occ_i_ref.1, f32[2]{0:T(128)} %occ_j_ref.1), custom_call_target="tpu_custom_call" | custom-call | tf_op jit(solution)/shard_map/pair_exchange/pallas_call | solution.py:333
  247.2 10.1 %last_block.1 = f32[1024,2048]{1,0:T(8,128)} custom-call(f32[1024,2048]{1,0:T(8,128)} %get-tuple-element.8.part_ref, bf16[1024,768]{1,0:T(8,128)(2,1)} %get-tuple-element.9.amp_ref, bf16[768,2048]{1,0:T(8,128)(2,1)} %get-tuple-element.10.j_ref), custom_call_target="tpu_custom_call" | custom-call | tf_op jit(solution)/shard_map/last_block/pallas_call | solution.py:369
